TPU v7x, 32 devices: a whole 2x2x4 slice. The times are simulated.
32 devices in a mesh: row: 8 (over z, x), rep: 4 (over y, core).
Axes of the slice: x: 2, y: 2, z: 4, core: 2. Of those that a mesh axis runs over, the one named last changes fastest.
Arguments:
- features: bfloat16 [16384, 4096], P('row'), may hold values from -6 to 6
- coefficients: bfloat16 [4096, 512], P('row', 'rep'), may hold values from -0.1875 to 0.1875
- multiplicity: int32 [16384, 512], P('row', 'rep'), may hold values from 0 to 3
- treated: int32 [16384], P('row'), may hold values from 0 to 1
- outcome: int32 [16384], P('row'), may hold values from 0 to 1
- offset: float32 [16384], P('row'), may hold values from -4 to 4
- trim_low: int32 [512], P('rep'), may hold values from -768 to -256
- trim_high: int32 [512], P('rep'), may hold values from 256 to 768
Outputs:
- new_coefficients: float32 [4096, 512], P('row', 'rep')
- score: float32 [4096, 512], P('row', 'rep')
- effect: float32 [2, 4, 128], P(None, 'rep', 'row')
All inputs are finite; a program needn't handle non-finite values.
Results may differ from a plain program's by a relative error of at most 0.003.
Values may be sent and summed in bfloat16 or wider, within the bound.
A program may use at most 128 MiB of HBM per device.

v0:
```python
import jax
import jax.numpy as jnp
from jax import lax
from jax.sharding import PartitionSpec as P

REFIT_ITERS = 2


def newton_step(a_coef, c_coef, stats):
    ga = stats[0]
    gc = stats[1]
    s_all = stats[2]
    s_tr = stats[3]
    h11 = s_all + 1.0
    h22 = s_tr + 1.0
    det = h11 * h22 - s_tr * s_tr
    return (a_coef + (h22 * ga - s_tr * gc) / det, c_coef + (h11 * gc - s_tr * ga) / det)


def column_stats(a_coef, c_coef, ipw_t, treat, target, offset):
    prob = jax.nn.sigmoid(a_coef[:, None] + c_coef[:, None] * treat[None, :] + offset[None, :])
    res = ipw_t * (target[None, :] - prob)
    cur = ipw_t * prob * (1.0 - prob)
    return jnp.stack(
        [
            jnp.sum(res, axis=1),
            jnp.sum(res * treat[None, :], axis=1),
            jnp.sum(cur, axis=1),
            jnp.sum(cur * treat[None, :], axis=1),
        ]
    )


def local(features, coefficients, multiplicity, treated, outcome, offset, trim_low, trim_high):
    rep_block = coefficients.shape[1]
    cols = features
    logits = jnp.dot(
        cols,
        lax.all_gather(coefficients, "row", axis=0, tiled=True),
        preferred_element_type=jnp.float32,
    )
    low = trim_low.astype(jnp.float32) / 256.0
    high = trim_high.astype(jnp.float32) / 256.0
    prop = jax.nn.sigmoid(jnp.minimum(jnp.maximum(logits, low[None, :]), high[None, :]))
    weight = multiplicity.astype(jnp.float32)
    treat = treated.astype(jnp.float32)
    target = outcome.astype(jnp.float32)
    resid = (weight * (treat[:, None] - prop)).astype(jnp.bfloat16)
    curv = (weight * prop * (1.0 - prop)).astype(jnp.bfloat16)
    contract = (((0,), (0,)), ((), ()))
    cols = features
    grad = lax.psum_scatter(
        lax.dot_general(cols, resid, contract, preferred_element_type=jnp.float32),
        "row",
        scatter_dimension=0,
        tiled=True,
    )
    cols = features
    squared = (cols.astype(jnp.float32) * cols.astype(jnp.float32)).astype(jnp.bfloat16)
    hess = lax.psum_scatter(
        lax.dot_general(squared, curv, contract, preferred_element_type=jnp.float32),
        "row",
        scatter_dimension=0,
        tiled=True,
    )
    new_coefficients = coefficients.astype(jnp.float32) + grad / (hess + 1.0)
    score = grad / jnp.sqrt(hess + 1.0)
    prop_t = prop.T
    weight_t = weight.T
    ipw_t = weight_t * (treat[None, :] / prop_t + (1.0 - treat[None, :]) / (1.0 - prop_t))
    owned = rep_block // lax.axis_size("row")
    side = jnp.stack([treat, target, offset])
    side_all = lax.all_gather(side, "row", axis=1, tiled=True)
    mine = lax.all_to_all(ipw_t, "row", split_axis=0, concat_axis=1, tiled=True)
    a_coef = jnp.zeros((owned,), jnp.float32)
    c_coef = jnp.zeros((owned,), jnp.float32)
    for step in range(REFIT_ITERS):
        stats = column_stats(a_coef, c_coef, mine, side_all[0], side_all[1], side_all[2])
        a_coef, c_coef = newton_step(a_coef, c_coef, stats)
    result = jnp.stack([a_coef, c_coef])
    effect = result.reshape(2, 1, owned)
    return (new_coefficients, score, effect)


def solution(mesh):
    return jax.shard_map(
        local,
        mesh=mesh,
        in_specs=(
            P("row", None),
            P("row", "rep"),
            P("row", "rep"),
            P("row"),
            P("row"),
            P("row"),
            P("rep"),
            P("rep"),
        ),
        out_specs=(P("row", "rep"), P("row", "rep"), P(None, "rep", "row")),
        check_vma=False,
    )
```

profile of v0, /device:TPU:0, one launch (start us, length us, event | category | flops | bytes accessed | tf_op | source)
XLA Modules:
  0.0 235.5 jit_solution(13237240451449031860)
XLA Ops:
  7.2 0.0 all-gather.2.cloned.1.call-start
  7.2 0.7 all-gather.2.cloned.1.call-update
  7.9 0.0 reduce-scatter.3.cloned.1.call-start
  7.9 0.7 convert_element_type.33
  8.6 1.6 copy.12
  10.2 0.7 convert_multiply_fusion
  10.9 0.7 broadcast_subtract_fusion.1
  11.6 41.4 %all-gather.2.cloned.1.call-done = bf16[4096,128]{1,0:T(8,128)(2,1)} async-done(((bf16[512,128]{1,0:T(8,128)(2,1)}), bf16[4096,128]{1,0:T(8,128)(2,1)}) %all-gather.2.cloned.1.call-update) | async-done | bytes 1048592 | tf_op jit(solution)/shard_map/all_gather | solution.py:39
  53.0 12.9 %add_multiply_fusion = (f32[2048,128]{0,1:T(8,128)}, f32[2048,128]{0,1:T(8,128)S(1)}) fusion(s32[2048,128]{0,1:T(8,128)S(1)} %copy.12, f32[2048]{0:T(1024)S(1)} %broadcast_subtract_fusion.1, f32[2048]{0:T(1024)S(1)} %convert_element_type.33, f32[128]{0:T(128)S(1)} %get-tuple-element.31, f32[128]{0:T(128)S(1)} %get-tuple-element.32, ...), kind=kOutput, calls=%fused_computation.14 | convolution fusion | flops 2150367232 | bytes 20988928 | tf_op jit(solution)/shard_map/dot_general | solution.py:37
  65.9 9.5 %convolution_bitcast_fusion = f32[4096,128]{0,1:T(8,128)} fusion(bf16[2048,4096]{1,0:T(8,128)(2,1)} %param.8, s32[2048,128]{0,1:T(8,128)S(1)} %copy.12, f32[2048]{0:T(1024)S(1)} %convert_element_type.33, f32[2048,128]{0,1:T(8,128)S(1)} %get-tuple-element.30), kind=kOutput, calls=%fused_computation.2 | convolution fusion | flops 2148794368 | bytes 20979712 | tf_op jit(solution)/shard_map/dot_general | solution.py:53
  75.4 0.0 reduce-scatter.3.cloned.1.call-update
  75.4 0.0 copy-start
  75.5 0.0 copy-start.2
  75.5 0.0 copy-start.1
  75.5 0.0 reduce-scatter.5.cloned.1.call-start
  75.5 10.4 %fusion = f32[4096,128]{0,1:T(8,128)} fusion(bf16[2048,4096]{1,0:T(8,128)(2,1)} %param.8, s32[2048,128]{0,1:T(8,128)S(1)} %copy.12, f32[2048,128]{0,1:T(8,128)S(1)} %get-tuple-element.30), kind=kOutput, calls=%fused_computation.1 | convolution fusion | flops 2174222336 | bytes 20971520 | tf_op jit(solution)/shard_map/dot_general | solution.py:61
  86.0 0.0 reduce-scatter.5.cloned.1.call-update
  86.0 3.6 %all-to-all-start = ((f32[8,16,2048]{2,1,0:T(8,128)}), f32[8,16,2048]{2,1,0:T(8,128)S(1)}, u32[]{:S(2)}, u32[]{:S(2)}) async-start(f32[8,16,2048]{2,1,0:T(8,128)} %bitcast.2), calls=%async_computation.2 | async-start | bytes 2097152 | tf_op jit(solution)/shard_map/all_to_all | solution.py:74
  89.6 0.0 copy-done
  89.6 0.1 copy.11
  89.7 0.0 copy-done.2
  89.7 0.0 copy-done.1
  89.8 56.3 %all_gather.7 = f32[3,16384]{1,0:T(4,128)S(1)} all-gather(f32[3,2048]{1,0:T(4,128)S(1)} %pad_maximum_fusion), channel_id=1, replica_groups=mesh['row'=8,'rep'=4] {'row'}, dimensions={1}, use_global_device_ids=true | all-gather | bytes 221184 | tf_op jit(solution)/shard_map/all_gather | solution.py:73
  146.1 0.5 slice_reduce_fusion.2
  146.7 0.0 all-to-all-done
  146.7 0.7 fusion.8
  147.4 0.6 bitcast_multiply_fusion
  148.0 0.5 fusion.25
  148.5 0.6 pad_maximum_fusion.1
  149.1 6.5 %reduce-scatter.3.cloned.1.call-done = f32[512,128]{0,1:T(8,128)} async-done(((f32[4096,128]{0,1:T(8,128)}), f32[512,128]{0,1:T(8,128)}) %reduce-scatter.3.cloned.1.call-update) | async-done | bytes 262160 | tf_op jit(solution)/shard_map/reduce_scatter | solution.py:52
  155.6 70.6 %reduce-scatter.5.cloned.1.call-done = f32[512,128]{0,1:T(8,128)} async-done(((f32[4096,128]{0,1:T(8,128)}), f32[512,128]{0,1:T(8,128)}) %reduce-scatter.5.cloned.1.call-update) | async-done | bytes 262160 | tf_op jit(solution)/shard_map/reduce_scatter | solution.py:60
  226.2 1.1 rsqrt_multiply_fusion
  227.3 0.8 copy.14
  228.1 0.8 copy.15
  (9 shorter events, 0.2 us)
Async XLA Ops:
  7.2 45.9 %all-gather.2.cloned.1.call-start = ((), (), s32[]{:S(2)}) async-start(), calls=%async_computation.3 | async-start | bytes 1179648 | tf_op jit(solution)/shard_map/all_gather | solution.py:39
  7.9 147.7 %reduce-scatter.3.cloned.1.call-start = ((), (), s32[]{:S(2)}) async-start(), calls=%async_computation.4 | async-start | bytes 2359296 | tf_op jit(solution)/shard_map/reduce_scatter | solution.py:52
  75.4 14.1 %copy-start = (bf16[512,128]{1,0:T(8,128)(2,1)S(1)}, bf16[512,128]{1,0:T(8,128)(2,1)}, u32[]{:S(2)}) copy-start(bf16[512,128]{1,0:T(8,128)(2,1)} %param.9) | copy-start | bytes 393220
  75.5 14.2 %copy-start.2 = (s32[2048]{0:T(1024)S(1)}, s32[2048]{0:T(1024)}, u32[]{:S(2)}) copy-start(s32[2048]{0:T(1024)} %param.12) | copy-start | bytes 24580
  75.5 14.3 %copy-start.1 = (f32[2048]{0:T(1024)S(1)}, f32[2048]{0:T(1024)}, u32[]{:S(2)}) copy-start(f32[2048]{0:T(1024)} %param.13) | copy-start | bytes 24580
  75.5 150.7 %reduce-scatter.5.cloned.1.call-start = ((), (), s32[]{:S(2)}) async-start(), calls=%async_computation.5 | async-start | bytes 2359296 | tf_op jit(solution)/shard_map/reduce_scatter | solution.py:60
  86.0 60.7 %all-to-all-start = ((f32[8,16,2048]{2,1,0:T(8,128)}), f32[8,16,2048]{2,1,0:T(8,128)S(1)}, u32[]{:S(2)}, u32[]{:S(2)}) async-start(f32[8,16,2048]{2,1,0:T(8,128)} %bitcast.2), calls=%async_computation.2 | async-start | bytes 2097152 | tf_op jit(solution)/shard_map/all_to_all | solution.py:74
Sparse Core Ops, SparseCore 0:
  10.1 42.8 all-gather.1
  75.6 79.9 reduce-scatter.2
  159.1 67.0 reduce-scatter.4
where the time goes:
time: 236 us; the launch traced here: 235 us
  waiting for transfers between devices  119 us (50%)
  blocking collectives  56.3 us (24%)
  matrix products  32.8 us (14%)
  between operations  13.9 us (6%)
  other arithmetic  5.6 us (2%)
  local copies, waits for them, and re-layouts  3.92 us (2%)
  starting transfers between devices  3.69 us (2%)
    reduce_scatter x1, waiting for transfers between devices, local(): lax.psum_scatter(lax.dot_general(squared, curv, contract, preferred_eleme...  70.6 us
    all_gather x1, blocking collectives, local(): side_all = lax.all_gather(side, 'row', axis=1, tiled=True)  56.3 us
    all_gather x1, waiting for transfers between devices, local(): lax.all_gather(coefficients, 'row', axis=0, tiled=True)  41.4 us
    dot_general x1, matrix products, local(): jnp.dot(cols, lax.all_gather(coefficients, 'row', axis=0, tiled=True), pr...  12.9 us
    dot_general x1, matrix products, local(): lax.dot_general(squared, curv, contract, preferred_element_type=jnp.float32)  10.4 us
    dot_general x1, matrix products, local(): lax.dot_general(cols, resid, contract, preferred_element_type=jnp.float32)  9.49 us
    reduce_scatter x1, waiting for transfers between devices, local(): lax.psum_scatter(lax.dot_general(cols, resid, contract, preferred_element...  6.49 us
  transfers between devices with their start and end apart: 4, of which 3 were waited for; matrix products, arithmetic and copies ran while one was open for 7% of the time, Pallas kernels for 0%

commit v1 on v0

v1 whole, which is shorter than its diff:
```python
import functools

import jax
import jax.numpy as jnp
from jax import lax
from jax.experimental import pallas as pl
from jax.experimental.pallas import tpu as pltpu
from jax.sharding import PartitionSpec as P

REFIT_ITERS = 2
TILE = 128
F32 = jnp.float32
BF16 = jnp.bfloat16


def newton_step(a_coef, c_coef, stats):
    ga = stats[0:1]
    gc = stats[1:2]
    s_all = stats[2:3]
    s_tr = stats[3:4]
    h11 = s_all + 1.0
    h22 = s_tr + 1.0
    det = h11 * h22 - s_tr * s_tr
    return (a_coef + (h22 * ga - s_tr * gc) / det, c_coef + (h11 * gc - s_tr * ga) / det)


def kernel(
    n,
    feat_hbm,
    mult_hbm,
    coef_ref,
    side_ref,
    bounds_ref,
    new_ref,
    score_ref,
    eff_ref,
    feat,
    mult,
    coef_all,
    acc,
    ipw,
    resid,
    curv,
    keep,
    xsend,
    xrecv,
    zsend,
    zrecv,
    sums,
    stat_send,
    stat_recv,
    feat_sem,
    mult_sem,
    ag_send,
    ag_fwd,
    ag_recv,
    x_send,
    x_recv,
    z_send,
    z_recv,
    st_send,
    st_recv,
):
    outer = n // 2
    rep, width = acc.shape
    cols = coef_ref.shape[0]
    tiles = width // TILE
    me = lax.axis_index("row")
    mo = me // 2
    mx = lax.rem(me, 2)
    px = 1 - mx
    partner = 2 * mo + px

    def block(o, x):
        return 2 * o + x

    def shifted(i):
        return lax.rem(mo + i, outer)

    def behind(i):
        return lax.rem(mo - i + outer, outer)

    def remote(src, dst, send, recv, row):
        return pltpu.make_async_remote_copy(
            src_ref=src,
            dst_ref=dst,
            send_sem=send,
            recv_sem=recv,
            device_id={"row": row},
            device_id_type=pl.DeviceIdType.MESH,
        )

    def feat_copy(b):
        start = pl.multiple_of(b * cols, cols)
        return pltpu.make_async_copy(feat_hbm.at[:, pl.ds(start, cols)], feat.at[b], feat_sem.at[b])

    @pl.loop(0, outer)
    def _(i):
        o = behind(i)
        feat_copy(block(o, mx)).start()
        feat_copy(block(o, px)).start()

    mult_copy = pltpu.make_async_copy(mult_hbm, mult, mult_sem)
    mult_copy.start()

    barrier = pltpu.get_barrier_semaphore()
    for j in range(1, n):
        pl.semaphore_signal(
            barrier,
            inc=1,
            device_id={"row": lax.rem(me + j, n)},
            device_id_type=pl.DeviceIdType.MESH,
        )
    coef_all[me] = coef_ref[...].astype(F32).T.astype(BF16)
    pl.semaphore_wait(barrier, n - 1)

    def outer_copy(i):
        return remote(coef_all.at[me], coef_all.at[me], ag_send.at[i], ag_recv.at[me], block(shifted(i), mx))

    def forward_copy(o):
        b = block(o, mx)
        return remote(coef_all.at[b], coef_all.at[b], ag_fwd.at[o], ag_recv.at[b], partner)

    def coef_wait(b):
        remote(coef_all.at[b], coef_all.at[b], ag_fwd.at[0], ag_recv.at[b], partner).wait_recv()

    forward_copy(mo).start()

    @pl.loop(1, outer)
    def _(i):
        outer_copy(i).start()

    def logits_of(b, first):
        feat_copy(b).wait()
        part = lax.dot_general(
            coef_all[b], feat[b], (((1,), (1,)), ((), ())), preferred_element_type=F32
        )
        if first:
            acc[...] = part
        else:
            acc[...] += part

    logits_of(me, True)

    @pl.loop(1, outer)
    def _(i):
        o = behind(i)
        b = block(o, mx)
        coef_wait(b)
        forward_copy(o).start()
        logits_of(b, False)
        q = block(behind(i - 1), px)
        coef_wait(q)
        logits_of(q, False)

    last = block(behind(outer - 1), px)
    coef_wait(last)
    logits_of(last, False)

    low = jnp.broadcast_to(bounds_ref[0:1, :], (TILE, rep)).T
    high = jnp.broadcast_to(bounds_ref[1:2, :], (TILE, rep)).T
    mult_copy.wait()

    def add_sums(weighted, prob, treat, target):
        res = weighted * (target - prob)
        cur = weighted * (prob * (1.0 - prob))
        sums[0] += res
        sums[1] += res * treat
        sums[2] += cur
        sums[3] += cur * treat

    sums[...] = jnp.zeros_like(sums)

    @pl.loop(0, tiles)
    def _(t):
        start = pl.multiple_of(t * TILE, TILE)
        at = pl.ds(start, TILE)
        logit = jnp.minimum(jnp.maximum(acc[:, at], low), high)
        prop = 1.0 / (1.0 + jnp.exp(-logit))
        weight = mult[at, :].astype(F32).T
        treat = side_ref[0:1, at]
        target = side_ref[1:2, at]
        offset = side_ref[2:3, at]
        resid[:, at] = (weight * (treat - prop)).astype(BF16)
        curv[:, at] = (weight * prop * (1.0 - prop)).astype(BF16)
        weighted = weight * (1.0 + jnp.exp(jnp.where(treat > 0.5, -logit, logit)))
        ipw[:, at] = weighted
        add_sums(weighted, 1.0 / (1.0 + jnp.exp(-offset)), treat, target)

    def stat_copy(it, j):
        to = lax.rem(me + j, n)
        return remote(stat_send.at[it], stat_recv.at[it, me], st_send.at[it, j], st_recv.at[it, me], to)

    def send_stats(it):
        for k in range(4):
            stat_send[it, k : k + 1, :] = jnp.sum(sums[k].T, axis=0, keepdims=True)
        stat_send[it, 4:8, :] = jnp.zeros((4, rep), F32)
        stat_recv[it, me] = stat_send[it]
        @pl.loop(1, n)
        def _(j):
            stat_copy(it, j).start()

    def total_stats(it):
        @pl.loop(1, n)
        def _(j):
            src = lax.rem(me + j, n)
            remote(stat_send.at[it], stat_recv.at[it, src], st_send.at[it, j], st_recv.at[it, src], src).wait_recv()
            stat_copy(it, j).wait_send()

        return jnp.sum(stat_recv[it], axis=0)

    send_stats(0)

    def x_copy(o, k):
        return remote(xsend.at[o, k], xrecv.at[o, k], x_send.at[o, k], x_recv.at[o, k], partner)

    def z_copy(o, k):
        return remote(zsend.at[o, k], zrecv.at[mo, k], z_send.at[o, k], z_recv.at[mo, k], block(o, mx))

    def products(b, k):
        if k == 0:
            return jnp.dot(resid[...], feat[b], preferred_element_type=F32)
        wide = feat[b].astype(F32)
        return jnp.dot(curv[...], (wide * wide).astype(BF16), preferred_element_type=F32)

    def compute(o):
        for k in range(2):
            xsend[o, k] = products(block(o, px), k).astype(BF16)
            x_copy(o, k).start()
        for k in range(2):
            keep[o, k] = products(block(o, mx), k)

    def pass_on(o):
        for k in range(2):
            x_copy(o, k).wait_recv()
            zsend[o, k] = (keep[o, k] + xrecv[o, k].astype(F32)).astype(BF16)
            z_copy(o, k).start()

    compute(shifted(1))

    @pl.loop(2, outer + 1)
    def _(i):
        compute(shifted(i))
        pass_on(shifted(i - 1))

    zero = jnp.zeros((1, rep), F32)
    a_row, c_row = newton_step(zero, zero, total_stats(0))
    a_wide = jnp.broadcast_to(a_row, (TILE, rep)).T
    c_wide = jnp.broadcast_to(c_row, (TILE, rep)).T
    sums[...] = jnp.zeros_like(sums)

    @pl.loop(0, tiles)
    def _(t):
        start = pl.multiple_of(t * TILE, TILE)
        at = pl.ds(start, TILE)
        treat = side_ref[0:1, at]
        target = side_ref[1:2, at]
        offset = side_ref[2:3, at]
        prob = 1.0 / (1.0 + jnp.exp(-(a_wide + c_wide * treat + offset)))
        add_sums(ipw[:, at], prob, treat, target)

    send_stats(1)

    for k in range(2):
        x_copy(mo, k).wait_recv()
        keep[mo, k] = keep[mo, k] + xrecv[mo, k].astype(F32)

    @pl.loop(1, outer)
    def _(i):
        o = behind(i)
        for k in range(2):
            remote(zsend.at[o, k], zrecv.at[o, k], z_send.at[o, k], z_recv.at[o, k], block(o, mx)).wait_recv()
            keep[mo, k] = keep[mo, k] + zrecv[o, k].astype(F32)

    grad = keep[mo, 0].T
    hess = keep[mo, 1].T + 1.0
    new_ref[...] = coef_ref[...].astype(F32) + grad / hess
    score_ref[...] = grad / jnp.sqrt(hess)

    a_row, c_row = newton_step(a_row, c_row, total_stats(1))
    eff_ref[0:1, :] = a_row
    eff_ref[1:2, :] = c_row

    @pl.loop(0, outer)
    def _(o):
        forward_copy(o).wait_send()
        for k in range(2):
            x_copy(o, k).wait_send()

    @pl.loop(1, outer)
    def _(i):
        outer_copy(i).wait_send()
        for k in range(2):
            z_copy(shifted(i), k).wait_send()


def local(n, features, coefficients, multiplicity, treated, outcome, offset, trim_low, trim_high):
    rows, depth = features.shape
    cols, rep = coefficients.shape
    outer = n // 2
    side = jnp.stack([treated.astype(F32), outcome.astype(F32), offset])
    bounds = jnp.stack([trim_low, trim_high]).astype(F32) / 256.0
    anywhere = pl.BlockSpec(memory_space=pl.ANY)
    vmem = pl.BlockSpec(memory_space=pltpu.VMEM)
    dma = pltpu.SemaphoreType.DMA
    new_coefficients, score, eff = pl.pallas_call(
        functools.partial(kernel, n),
        out_shape=(
            jax.ShapeDtypeStruct((cols, rep), F32),
            jax.ShapeDtypeStruct((cols, rep), F32),
            jax.ShapeDtypeStruct((2, rep), F32),
        ),
        in_specs=[anywhere, anywhere, vmem, vmem, vmem],
        out_specs=(vmem, vmem, vmem),
        scratch_shapes=[
            pltpu.VMEM((n, rows, cols), BF16),
            pltpu.VMEM((rows, rep), jnp.int32),
            pltpu.VMEM((n, rep, cols), BF16),
            pltpu.VMEM((rep, rows), F32),
            pltpu.VMEM((rep, rows), F32),
            pltpu.VMEM((rep, rows), BF16),
            pltpu.VMEM((rep, rows), BF16),
            pltpu.VMEM((outer, 2, rep, cols), F32),
            pltpu.VMEM((outer, 2, rep, cols), BF16),
            pltpu.VMEM((outer, 2, rep, cols), BF16),
            pltpu.VMEM((outer, 2, rep, cols), BF16),
            pltpu.VMEM((outer, 2, rep, cols), BF16),
            pltpu.VMEM((4, rep, TILE), F32),
            pltpu.VMEM((REFIT_ITERS, 8, rep), F32),
            pltpu.VMEM((REFIT_ITERS, n, 8, rep), F32),
            dma((n,)),
            dma(()),
            dma((outer,)),
            dma((outer,)),
            dma((n,)),
            dma((outer, 2)),
            dma((outer, 2)),
            dma((outer, 2)),
            dma((outer, 2)),
            dma((REFIT_ITERS, n)),
            dma((REFIT_ITERS, n)),
        ],
        compiler_params=pltpu.CompilerParams(
            collective_id=0, has_side_effects=True, vmem_limit_bytes=52 * 1024 * 1024
        ),
        name="propensity",
    )(features, multiplicity, coefficients, side, bounds)
    owned = rep // n
    mine = lax.dynamic_slice_in_dim(eff, lax.axis_index("row") * owned, owned, axis=1)
    return (new_coefficients, score, mine.reshape(2, 1, owned))


def solution(mesh):
    return jax.shard_map(
        functools.partial(local, mesh.shape["row"]),
        mesh=mesh,
        in_specs=(
            P("row", None),
            P("row", "rep"),
            P("row", "rep"),
            P("row"),
            P("row"),
            P("row"),
            P("rep"),
            P("rep"),
        ),
        out_specs=(P("row", "rep"), P("row", "rep"), P(None, "rep", "row")),
        check_vma=False,
    )
```

time: 236 us -> 63.2 us (0.27)
  waiting for transfers between devices: 119 us -> 0 us
  blocking collectives: 56.3 us -> 0 us
  Pallas kernels: 0 us -> 55.3 us
  matrix products: 32.8 us -> 0 us
  between operations: 13.9 us -> 0.65 us
  starting transfers between devices: 3.69 us -> 0 us
  other arithmetic: 5.6 us -> 2.8 us
    reduce_scatter x2 -> x0, waiting for transfers between devices: 77.1 us -> none  [the longest x1 70.6 us: local(): lax.psum_scatter(lax.dot_general(squared, curv, contract, preferred_eleme...]
    all_gather x1 -> x0, blocking collectives: 56.3 us -> none  [local(): side_all = lax.all_gather(side, 'row', axis=1, tiled=True)]
    pallas_call x0 -> x1, Pallas kernels: none -> 55.3 us  [local(): pl.pallas_call(functools.partial(kernel, n), out_shape=(jax.ShapeDtypeStr...]
    all_gather x1 -> x0, waiting for transfers between devices: 41.4 us -> none  [local(): lax.all_gather(coefficients, 'row', axis=0, tiled=True)]
    dot_general x3 -> x0, matrix products: 32.8 us -> none  [the longest x1 12.9 us: local(): jnp.dot(cols, lax.all_gather(coefficients, 'row', axis=0, tiled=True), pr...]
    all_to_all x1 -> x0, starting transfers between devices: 3.57 us -> none  [local(): mine = lax.all_to_all(ipw_t, 'row', split_axis=0, concat_axis=1, tiled=True)]
  transfers between devices with their start and end apart: 4 -> 0, of which waited for: 3 -> 0; matrix products, arithmetic and copies ran while one was open for 7% -> 0% of each run, Pallas kernels for 0% -> 0%
where the time goes in v1:
time: 63.2 us; the launch traced here: 62.9 us
  Pallas kernels  55.3 us (88%)
  local copies, waits for them, and re-layouts  4.17 us (7%)
  other arithmetic  2.8 us (4%)
  between operations  0.65 us (1%)
    pallas_call x1, Pallas kernels, local(): pl.pallas_call(functools.partial(kernel, n), out_shape=(jax.ShapeDtypeStr...  55.3 us
    unnamed x6, local copies, waits for them, and re-layouts  3.53 us
    convert_element_type x2, other arithmetic, local(): side = jnp.stack([treated.astype(F32), outcome.astype(F32), offset])  1.4 us

profile of v1, /device:TPU:0, one launch (start us, length us, event | category | flops | bytes accessed | tf_op | source)
XLA Modules:
  0.0 62.9 jit_solution(18257195300871900279)
XLA Ops:
  0.6 0.7 %convert_element_type.9 = f32[2048]{0:T(1024)S(1)} convert(s32[2048]{0:T(1024)} %param.11) | non-fusion elementwise | flops 2048 | bytes 16384 | tf_op jit(solution)/shard_map/convert_element_type | solution.py:301
  1.3 0.7 %convert_element_type.10 = f32[2048]{0:T(1024)S(1)} convert(s32[2048]{0:T(1024)} %param.12) | non-fusion elementwise | flops 2048 | bytes 16384 | tf_op jit(solution)/shard_map/convert_element_type | solution.py:301
  2.0 0.7 %pad_maximum_fusion.side_ref = f32[3,2048]{1,0:T(4,128)S(1)} fusion(f32[1,2048]{1,0:T(1,128)} %bitcast.10, f32[1,2048]{1,0:T(1,128)S(1)} %bitcast.9, f32[1,2048]{1,0:T(1,128)S(1)} %bitcast.8), kind=kLoop, calls=%fused_computation | loop fusion | flops 12288 | bytes 49152 | tf_op jit(solution)/shard_map/stack | solution.py:301
  2.8 0.7 %fusion.bounds_ref = f32[2,128]{1,0:T(2,128)S(1)} fusion(s32[1,128]{1,0:T(1,128)} %bitcast.12, s32[1,128]{1,0:T(1,128)} %bitcast.13), kind=kLoop, calls=%fused_computation.2 | loop fusion | flops 768 | bytes 2048 | tf_op jit(solution)/shard_map/div | solution.py:302
  3.4 0.0 copy-start
  3.4 1.2 %copy-done = s32[2048,128]{1,0:T(8,128)S(1)} copy-done((s32[2048,128]{1,0:T(8,128)S(1)}, s32[2048,128]{1,0:T(8,128)}, u32[]{:S(2)}) %copy-start) | copy-done | bytes 1048600
  4.7 0.0 copy-start.1
  4.7 0.9 %copy-done.1 = bf16[512,128]{1,0:T(8,128)(2,1)S(1)} copy-done((bf16[512,128]{1,0:T(8,128)(2,1)S(1)}, bf16[512,128]{1,0:T(8,128)(2,1)}, u32[]{:S(2)}) %copy-start.1) | copy-done | bytes 131096
  5.6 55.3 %propensity.1 = (f32[512,128]{1,0:T(8,128)S(1)}, f32[512,128]{1,0:T(8,128)S(1)}, f32[2,128]{1,0:T(2,128)S(1)}) custom-call(bf16[2048,4096]{1,0:T(8,128)(2,1)} %feat_hbm.1, s32[2048,128]{1,0:T(8,128)S(1)} %copy-done, bf16[512,128]{1,0:T(8,128)(2,1)S(1)} %copy-done.1, f32[3,2048]{1,0:T(4,128)S(1)} %pad_maximum_fusion.side_ref, f32[2,128]{1,0:T(2,128)S(1)} %fusion.bounds_ref), custom_call_target="tpu_custom_call" | custom-call | tf_op jit(solution)/shard_map/propensity/pallas_call | solution.py:306
  60.9 0.6 %constant_dynamic-slice_fusion = f32[2,16]{1,0:T(2,128)} fusion(f32[2,128]{1,0:T(2,128)S(1)} %get-tuple-element.8, s32[]{:T(128)S(6)} %select_n.3), kind=kLoop, calls=%fused_computation.3 | loop fusion | bytes 260 | tf_op jit(solution)/shard_map/dynamic_slice | solution.py:349
  61.5 0.7 %copy.14 = f32[512,128]{1,0:T(8,128)} copy(f32[512,128]{1,0:T(8,128)S(1)} %get-tuple-element.15) | data formatting | bytes 524288
  62.2 0.7 %copy.15 = f32[512,128]{1,0:T(8,128)} copy(f32[512,128]{1,0:T(8,128)S(1)} %get-tuple-element.16) | data formatting | bytes 524288
Async XLA Ops:
  3.4 1.2 %copy-start = (s32[2048,128]{1,0:T(8,128)S(1)}, s32[2048,128]{1,0:T(8,128)}, u32[]{:S(2)}) copy-start(s32[2048,128]{1,0:T(8,128)} %mult_hbm.1) | copy-start | bytes 3145732
  4.7 0.9 %copy-start.1 = (bf16[512,128]{1,0:T(8,128)(2,1)S(1)}, bf16[512,128]{1,0:T(8,128)(2,1)}, u32[]{:S(2)}) copy-start(bf16[512,128]{1,0:T(8,128)(2,1)} %coef_ref.1) | copy-start | bytes 393220

commit v2 on v1

v2 whole, which is shorter than its diff:
```python
import functools

import jax
import jax.numpy as jnp
from jax import lax
from jax.experimental import pallas as pl
from jax.experimental.pallas import tpu as pltpu
from jax.sharding import PartitionSpec as P

REFIT_ITERS = 2
TILE = 128
F32 = jnp.float32
BF16 = jnp.bfloat16


def newton_step(a_coef, c_coef, stats):
    ga = stats[0:1]
    gc = stats[1:2]
    s_all = stats[2:3]
    s_tr = stats[3:4]
    h11 = s_all + 1.0
    h22 = s_tr + 1.0
    det = h11 * h22 - s_tr * s_tr
    return (a_coef + (h22 * ga - s_tr * gc) / det, c_coef + (h11 * gc - s_tr * ga) / det)


def kernel(
    n,
    feat_hbm,
    mult_hbm,
    coef_hbm,
    treat_hbm,
    target_hbm,
    offset_hbm,
    low_hbm,
    high_hbm,
    grad_ref,
    hess_ref,
    eff_ref,
    feat,
    mult,
    coef,
    treat_ref,
    target_ref,
    offset_ref,
    low_ref,
    high_ref,
    coef_all,
    wide_weight,
    acc,
    ipw,
    resid,
    curv,
    keep,
    xsend,
    xrecv,
    zsend,
    zrecv,
    sums,
    stat_send,
    stat_recv,
    feat_sem,
    mult_sem,
    coef_sem,
    side_sem,
    ag_up,
    ag_down,
    ag_fwd,
    ag_recv,
    x_send,
    x_recv,
    z_send,
    z_recv,
    st_send,
    st_recv,
):
    outer = n // 2
    rep, width = acc.shape
    cols = coef.shape[0]
    tiles = width // TILE
    me = lax.axis_index("row")
    mo = me // 2
    mx = lax.rem(me, 2)
    px = 1 - mx
    partner = 2 * mo + px

    def block(o, x):
        return 2 * o + x

    low_side = 1 - (2 * mo) // outer
    near = low_side * mo + (1 - low_side) * (outer - 1 - mo)
    far = outer - 1 - near

    def target_of(i):
        j = i - (far - near)
        both = mo + (1 - 2 * lax.rem(j + 2 * outer, 2)) * (near - (j + 2 * outer) // 2 + outer)
        return jnp.where(j < 0, mo + (2 * low_side - 1) * (far - i), both)

    def remote(src, dst, send, recv, row):
        return pltpu.make_async_remote_copy(
            src_ref=src,
            dst_ref=dst,
            send_sem=send,
            recv_sem=recv,
            device_id={"row": row},
            device_id_type=pl.DeviceIdType.MESH,
        )

    def feat_copy(b):
        start = pl.multiple_of(b * cols, cols)
        return pltpu.make_async_copy(feat_hbm.at[:, pl.ds(start, cols)], feat.at[b], feat_sem.at[b])

    coef_copy = pltpu.make_async_copy(coef_hbm, coef, coef_sem)
    coef_copy.start()
    mult_copy = pltpu.make_async_copy(mult_hbm, mult, mult_sem)
    mult_copy.start()
    pairs = (
        (treat_hbm, treat_ref),
        (target_hbm, target_ref),
        (offset_hbm, offset_ref),
        (low_hbm, low_ref),
        (high_hbm, high_ref),
    )
    side_copies = [pltpu.make_async_copy(a, b, side_sem.at[i]) for i, (a, b) in enumerate(pairs)]
    for copy in side_copies:
        copy.start()

    barrier = pltpu.get_barrier_semaphore()
    for j in range(1, n):
        pl.semaphore_signal(
            barrier,
            inc=1,
            device_id={"row": lax.rem(me + j, n)},
            device_id_type=pl.DeviceIdType.MESH,
        )
    coef_copy.wait()
    coef_all[me] = coef[...].astype(F32).T.astype(BF16)
    pl.semaphore_wait(barrier, n - 1)

    def up_copy(o):
        b = block(o, mx)
        return remote(coef_all.at[b], coef_all.at[b], ag_up.at[o], ag_recv.at[b], block(mo + 1, mx))

    def down_copy(o):
        b = block(o, mx)
        return remote(coef_all.at[b], coef_all.at[b], ag_down.at[o], ag_recv.at[b], block(mo - 1, mx))

    def forward_copy(o):
        b = block(o, mx)
        return remote(coef_all.at[b], coef_all.at[b], ag_fwd.at[o], ag_recv.at[b], partner)

    def coef_wait(b):
        remote(coef_all.at[b], coef_all.at[b], ag_fwd.at[0], ag_recv.at[b], partner).wait_recv()

    has_up = mo + 1 < outer
    has_down = mo > 0

    @pl.when(has_up)
    def _():
        up_copy(mo).start()

    @pl.when(has_down)
    def _():
        down_copy(mo).start()

    forward_copy(mo).start()

    feat_copy(me).start()
    feat_copy(partner).start()

    @pl.loop(1, outer)
    def _(i):
        @pl.when(mo - i >= 0)
        def _():
            feat_copy(block(mo - i, mx)).start()
            feat_copy(block(mo - i, px)).start()

        @pl.when(mo + i < outer)
        def _():
            feat_copy(block(mo + i, mx)).start()
            feat_copy(block(mo + i, px)).start()

    mult_copy.wait()
    for copy in side_copies:
        copy.wait()

    @pl.loop(0, tiles)
    def _(t):
        at = pl.ds(pl.multiple_of(t * TILE, TILE), TILE)
        wide_weight[:, at] = mult[at, :].astype(F32).T

    def logits_of(b, first):
        feat_copy(b).wait()
        part = lax.dot_general(
            coef_all[b], feat[b], (((1,), (1,)), ((), ())), preferred_element_type=F32
        )
        if first:
            acc[...] = part
        else:
            acc[...] += part

    logits_of(me, True)

    def arrived(b):
        coef_wait(b)
        logits_of(b, False)

    @pl.loop(1, outer)
    def _(i):
        below = mo - i
        above = mo + i

        @pl.when(below >= 0)
        def _():
            coef_wait(block(below, mx))

            @pl.when(has_up)
            def _():
                up_copy(below).start()

            forward_copy(below).start()

        @pl.when(above < outer)
        def _():
            coef_wait(block(above, mx))

            @pl.when(has_down)
            def _():
                down_copy(above).start()

            forward_copy(above).start()

        @pl.when(below >= 0)
        def _():
            logits_of(block(below, mx), False)

        @pl.when(above < outer)
        def _():
            logits_of(block(above, mx), False)

        @pl.when(below + 1 >= 0)
        def _():
            arrived(block(below + 1, px))

        @pl.when(jnp.logical_and(above - 1 < outer, i > 1))
        def _():
            arrived(block(above - 1, px))

    @pl.when(mo == outer - 1)
    def _():
        arrived(block(0, px))

    @pl.when(mo == 0)
    def _():
        arrived(block(outer - 1, px))

    low = jnp.broadcast_to(low_ref[...].astype(F32) / 256.0, (TILE, rep)).T
    high = jnp.broadcast_to(high_ref[...].astype(F32) / 256.0, (TILE, rep)).T

    def add_sums(weighted, prob, treat, target):
        res = weighted * (target - prob)
        cur = weighted * (prob * (1.0 - prob))
        sums[0] += res
        sums[1] += res * treat
        sums[2] += cur
        sums[3] += cur * treat

    @pl.loop(0, tiles)
    def _(t):
        at = pl.ds(pl.multiple_of(t * TILE, TILE), TILE)
        logit = jnp.minimum(jnp.maximum(acc[:, at], low), high)
        prop = 1.0 / (1.0 + jnp.exp(-logit))
        weight = wide_weight[:, at]
        treat = treat_ref[:, at].astype(F32)
        resid[:, at] = (weight * (treat - prop)).astype(BF16)
        curv[:, at] = (weight * prop * (1.0 - prop)).astype(BF16)

    def first_sums():
        sums[...] = jnp.zeros_like(sums)

        @pl.loop(0, tiles)
        def _(t):
            at = pl.ds(pl.multiple_of(t * TILE, TILE), TILE)
            logit = jnp.minimum(jnp.maximum(acc[:, at], low), high)
            treat = treat_ref[:, at].astype(F32)
            target = target_ref[:, at].astype(F32)
            weighted = wide_weight[:, at] * (1.0 + jnp.exp(jnp.where(treat > 0.5, -logit, logit)))
            ipw[:, at] = weighted
            add_sums(weighted, 1.0 / (1.0 + jnp.exp(-offset_ref[:, at])), treat, target)

    def stat_copy(it, j):
        to = lax.rem(me + j, n)
        return remote(stat_send.at[it], stat_recv.at[it, me], st_send.at[it, j], st_recv.at[it, me], to)

    def send_stats(it):
        for k in range(4):
            stat_send[it, k : k + 1, :] = jnp.sum(sums[k].T, axis=0, keepdims=True)
        stat_send[it, 4:8, :] = jnp.zeros((4, rep), F32)
        stat_recv[it, me] = stat_send[it]
        @pl.loop(1, n)
        def _(j):
            stat_copy(it, j).start()

    def total_stats(it):
        @pl.loop(1, n)
        def _(j):
            src = lax.rem(me + j, n)
            remote(stat_send.at[it], stat_recv.at[it, src], st_send.at[it, j], st_recv.at[it, src], src).wait_recv()
            stat_copy(it, j).wait_send()

        return jnp.sum(stat_recv[it], axis=0)

    def x_copy(o, k):
        return remote(xsend.at[o, k], xrecv.at[o, k], x_send.at[o, k], x_recv.at[o, k], partner)

    def z_up(o, k):
        return remote(zsend.at[o, k], zrecv.at[o, k], z_send.at[o, k], z_recv.at[o, k], block(mo + 1, mx))

    def z_down(o, k):
        slot = jnp.where(o == mo - 1, outer, o)
        return remote(zsend.at[o, k], zrecv.at[slot, k], z_send.at[o, k], z_recv.at[slot, k], block(mo - 1, mx))

    def z_wait(slot, k):
        remote(zsend.at[0, k], zrecv.at[slot, k], z_send.at[0, k], z_recv.at[slot, k], partner).wait_recv()

    def products(b, k):
        if k == 0:
            return jnp.dot(resid[...], feat[b], preferred_element_type=F32)
        wide = feat[b].astype(F32)
        return jnp.dot(curv[...], (wide * wide).astype(BF16), preferred_element_type=F32)

    def compute(o):
        for k in range(2):
            xsend[o, k] = products(block(o, px), k).astype(BF16)
            x_copy(o, k).start()
        for k in range(2):
            keep[o, k] = products(block(o, mx), k)

    def add_in(o, slot, k):
        z_wait(slot, k)
        keep[o, k] += zrecv[slot, k].astype(F32)

    def pass_on(o):
        for k in range(2):
            x_copy(o, k).wait_recv()
            keep[o, k] += xrecv[o, k].astype(F32)

            @pl.when(jnp.logical_or(jnp.logical_and(o > mo, has_down), jnp.logical_and(o < mo, has_up)))
            def _():
                add_in(o, o, k)

            zsend[o, k] = keep[o, k].astype(BF16)

            @pl.when(o > mo)
            def _():
                z_up(o, k).start()

            @pl.when(o < mo)
            def _():
                z_down(o, k).start()

    compute(target_of(0))
    first_sums()
    send_stats(0)
    compute(target_of(1))

    @pl.loop(2, outer)
    def _(i):
        compute(target_of(i))

        @pl.when(i < outer - 1)
        def _():
            pass_on(target_of(i - 2))

    zero = jnp.zeros((1, rep), F32)
    a_row, c_row = newton_step(zero, zero, total_stats(0))
    a_wide = jnp.broadcast_to(a_row, (TILE, rep)).T
    c_wide = jnp.broadcast_to(c_row, (TILE, rep)).T
    sums[...] = jnp.zeros_like(sums)

    @pl.loop(0, tiles)
    def _(t):
        at = pl.ds(pl.multiple_of(t * TILE, TILE), TILE)
        treat = treat_ref[:, at].astype(F32)
        target = target_ref[:, at].astype(F32)
        offset = offset_ref[:, at]
        prob = 1.0 / (1.0 + jnp.exp(-(a_wide + c_wide * treat + offset)))
        add_sums(ipw[:, at], prob, treat, target)

    send_stats(1)

    for i in range(max(outer - 3, 0), outer - 1):
        pass_on(target_of(i))

    for k in range(2):
        x_copy(mo, k).wait_recv()
        keep[mo, k] += xrecv[mo, k].astype(F32)

        @pl.when(has_down)
        def _():
            add_in(mo, mo, k)

        @pl.when(has_up)
        def _():
            add_in(mo, outer, k)

    grad_ref[...] = keep[mo, 0].T
    hess_ref[...] = keep[mo, 1].T

    a_row, c_row = newton_step(a_row, c_row, total_stats(1))
    eff_ref[0:1, :] = a_row
    eff_ref[1:2, :] = c_row

    @pl.loop(0, outer)
    def _(o):
        forward_copy(o).wait_send()
        for k in range(2):
            x_copy(o, k).wait_send()

        @pl.when(has_up)
        def _():
            @pl.when(o <= mo)
            def _():
                up_copy(o).wait_send()

            @pl.when(o > mo)
            def _():
                for k in range(2):
                    z_up(o, k).wait_send()

        @pl.when(has_down)
        def _():
            @pl.when(o >= mo)
            def _():
                down_copy(o).wait_send()

            @pl.when(o < mo)
            def _():
                for k in range(2):
                    z_down(o, k).wait_send()


def local(n, features, coefficients, multiplicity, treated, outcome, offset, trim_low, trim_high):
    rows, depth = features.shape
    cols, rep = coefficients.shape
    outer = n // 2
    hbm = pl.BlockSpec(memory_space=pltpu.HBM)
    vmem = pl.BlockSpec(memory_space=pltpu.VMEM)
    dma = pltpu.SemaphoreType.DMA
    grad, hess, eff = pl.pallas_call(
        functools.partial(kernel, n),
        out_shape=(
            jax.ShapeDtypeStruct((cols, rep), F32),
            jax.ShapeDtypeStruct((cols, rep), F32),
            jax.ShapeDtypeStruct((2, rep), F32),
        ),
        in_specs=[hbm] * 8,
        out_specs=(vmem, vmem, vmem),
        scratch_shapes=[
            pltpu.VMEM((n, rows, cols), BF16),
            pltpu.VMEM((rows, rep), jnp.int32),
            pltpu.VMEM((cols, rep), BF16),
            pltpu.VMEM((1, rows), jnp.int32),
            pltpu.VMEM((1, rows), jnp.int32),
            pltpu.VMEM((1, rows), F32),
            pltpu.VMEM((1, rep), jnp.int32),
            pltpu.VMEM((1, rep), jnp.int32),
            pltpu.VMEM((n, rep, cols), BF16),
            pltpu.VMEM((rep, rows), F32),
            pltpu.VMEM((rep, rows), F32),
            pltpu.VMEM((rep, rows), F32),
            pltpu.VMEM((rep, rows), BF16),
            pltpu.VMEM((rep, rows), BF16),
            pltpu.VMEM((outer, 2, rep, cols), F32),
            pltpu.VMEM((outer, 2, rep, cols), BF16),
            pltpu.VMEM((outer, 2, rep, cols), BF16),
            pltpu.VMEM((outer, 2, rep, cols), BF16),
            pltpu.VMEM((outer + 1, 2, rep, cols), BF16),
            pltpu.VMEM((4, rep, TILE), F32),
            pltpu.VMEM((REFIT_ITERS, 8, rep), F32),
            pltpu.VMEM((REFIT_ITERS, n, 8, rep), F32),
            dma((n,)),
            dma(()),
            dma(()),
            dma((5,)),
            dma((outer,)),
            dma((outer,)),
            dma((outer,)),
            dma((n,)),
            dma((outer, 2)),
            dma((outer, 2)),
            dma((outer, 2)),
            dma((outer + 1, 2)),
            dma((REFIT_ITERS, n)),
            dma((REFIT_ITERS, n)),
        ],
        compiler_params=pltpu.CompilerParams(
            collective_id=0, has_side_effects=True, vmem_limit_bytes=63 * 1024 * 1024
        ),
        name="propensity",
    )(
        features,
        multiplicity,
        coefficients,
        treated.reshape(1, rows),
        outcome.reshape(1, rows),
        offset.reshape(1, rows),
        trim_low.reshape(1, rep),
        trim_high.reshape(1, rep),
    )
    hess = hess + 1.0
    new_coefficients = coefficients.astype(F32) + grad / hess
    score = grad / jnp.sqrt(hess)
    owned = rep // n
    mine = lax.dynamic_slice_in_dim(eff, lax.axis_index("row") * owned, owned, axis=1)
    return (new_coefficients, score, mine.reshape(2, 1, owned))


def solution(mesh):
    return jax.shard_map(
        functools.partial(local, mesh.shape["row"]),
        mesh=mesh,
        in_specs=(
            P("row", None),
            P("row", "rep"),
            P("row", "rep"),
            P("row"),
            P("row"),
            P("row"),
            P("rep"),
            P("rep"),
        ),
        out_specs=(P("row", "rep"), P("row", "rep"), P(None, "rep", "row")),
        check_vma=False,
    )
```

time: 63.2 us -> 54.9 us (0.87)
  Pallas kernels: 55.3 us -> 50.9 us
  local copies, waits for them, and re-layouts: 4.17 us -> 1.28 us
  other arithmetic: 2.8 us -> 1.89 us
    pallas_call x1, Pallas kernels: 55.3 us -> 50.9 us  [local(): pl.pallas_call(functools.partial(kernel, n), out_shape=(jax.ShapeDtypeStr...]
    unnamed x6 -> x2, local copies, waits for them, and re-layouts: 3.53 us -> 0.01 us
    convert_element_type x2 -> x0, other arithmetic: 1.4 us -> none  [local(): side = jnp.stack([treated.astype(F32), outcome.astype(F32), offset])]
    div x1, other arithmetic: 0.68 us -> 1.89 us  [local(): score = grad / jnp.sqrt(hess)]
    another operation x1 -> x0, other arithmetic: 0.72 us -> none  [local(): side = jnp.stack([treated.astype(F32), outcome.astype(F32), offset])]
    dynamic_slice x1, local copies, waits for them, and re-layouts: 0.64 us -> 1.27 us  [local(): lax.dynamic_slice_in_dim(eff, lax.axis_index('row') * owned, owned, axis=1)]
where the time goes in v2:
time: 54.9 us; the launch traced here: 54.7 us
  Pallas kernels  50.9 us (93%)
  other arithmetic  1.89 us (3%)
  local copies, waits for them, and re-layouts  1.28 us (2%)
  between operations  0.66 us (1%)
    pallas_call x1, Pallas kernels, local(): pl.pallas_call(functools.partial(kernel, n), out_shape=(jax.ShapeDtypeStr...  50.9 us
    div x1, other arithmetic, local(): score = grad / jnp.sqrt(hess)  1.89 us
    dynamic_slice x1, local copies, waits for them, and re-layouts, local(): lax.dynamic_slice_in_dim(eff, lax.axis_index('row') * owned, owned, axis=1)  1.27 us

profile of v2, /device:TPU:0, one launch (start us, length us, event | category | flops | bytes accessed | tf_op | source)
XLA Modules:
  0.0 54.7 jit_solution(15534199654640709423)
XLA Ops:
  0.6 0.0 copy-start
  0.6 50.9 %propensity.1 = (f32[512,128]{1,0:T(8,128)}, f32[512,128]{1,0:T(8,128)}, f32[2,128]{1,0:T(2,128)}) custom-call(bf16[2048,4096]{1,0:T(8,128)(2,1)} %feat_hbm.1, s32[2048,128]{1,0:T(8,128)} %mult_hbm.1, bf16[512,128]{1,0:T(8,128)(2,1)} %coef_hbm.1, s32[1,2048]{1,0:T(1,128)} %bitcast.8, s32[1,2048]{1,0:T(1,128)} %bitcast.9, f32[1,2048]{1,0:T(1,128)} %bitcast.10, ...), custom_call_target="tpu_custom_call" | custom-call | tf_op jit(solution)/shard_map/propensity/pallas_call | solution.py:450
  51.5 1.3 %constant_dynamic-slice_fusion = f32[2,16]{1,0:T(2,128)} fusion(f32[2,128]{1,0:T(2,128)} %get-tuple-element.8, s32[]{:T(128)S(6)} %select_n.3), kind=kLoop, calls=%fused_computation.2 | loop fusion | bytes 260 | tf_op jit(solution)/shard_map/dynamic_slice | solution.py:515
  52.8 0.0 copy-done
  52.8 1.9 %rsqrt_multiply_fusion = (f32[512,128]{1,0:T(8,128)}, f32[512,128]{1,0:T(8,128)}) fusion(f32[512,128]{1,0:T(8,128)} %get-tuple-element.6, f32[512,128]{1,0:T(8,128)} %get-tuple-element.7, bf16[512,128]{1,0:T(8,128)(2,1)S(1)} %copy-done), kind=kLoop, calls=%fused_computation | loop fusion | flops 327680 | bytes 1179648 | tf_op jit(solution)/shard_map/div | solution.py:513
Async XLA Ops:
  0.6 52.2 %copy-start = (bf16[512,128]{1,0:T(8,128)(2,1)S(1)}, bf16[512,128]{1,0:T(8,128)(2,1)}, u32[]{:S(2)}) copy-start(bf16[512,128]{1,0:T(8,128)(2,1)} %coef_hbm.1) | copy-start | bytes 393220

commit v3 on v2

--- a/solution.py
+++ b/solution.py
@@ -9,6 +9,7 @@
 
 REFIT_ITERS = 2
 TILE = 128
+PIECES = 2
 F32 = jnp.float32
 BF16 = jnp.bfloat16
 
@@ -134,36 +135,38 @@
             device_id_type=pl.DeviceIdType.MESH,
         )
     coef_copy.wait()
-    coef_all[me] = coef[...].astype(F32).T.astype(BF16)
+    coef_all[me] = coef[...].astype(F32).T.astype(BF16).reshape(coef_all.shape[1:])
     pl.semaphore_wait(barrier, n - 1)
 
-    def up_copy(o):
+    def gather_copy(o, h, send, row):
         b = block(o, mx)
-        return remote(coef_all.at[b], coef_all.at[b], ag_up.at[o], ag_recv.at[b], block(mo + 1, mx))
-
-    def down_copy(o):
-        b = block(o, mx)
-        return remote(coef_all.at[b], coef_all.at[b], ag_down.at[o], ag_recv.at[b], block(mo - 1, mx))
-
-    def forward_copy(o):
-        b = block(o, mx)
-        return remote(coef_all.at[b], coef_all.at[b], ag_fwd.at[o], ag_recv.at[b], partner)
-
-    def coef_wait(b):
-        remote(coef_all.at[b], coef_all.at[b], ag_fwd.at[0], ag_recv.at[b], partner).wait_recv()
+        return remote(coef_all.at[b, h], coef_all.at[b, h], send.at[o, h], ag_recv.at[b, h], row)
+
+    def up_copy(o, h):
+        return gather_copy(o, h, ag_up, block(mo + 1, mx))
+
+    def down_copy(o, h):
+        return gather_copy(o, h, ag_down, block(mo - 1, mx))
+
+    def forward_copy(o, h):
+        return gather_copy(o, h, ag_fwd, partner)
+
+    def coef_wait(b, h):
+        remote(coef_all.at[b, h], coef_all.at[b, h], ag_fwd.at[0, h], ag_recv.at[b, h], partner).wait_recv()
 
     has_up = mo + 1 < outer
     has_down = mo > 0
 
-    @pl.when(has_up)
-    def _():
-        up_copy(mo).start()
-
-    @pl.when(has_down)
-    def _():
-        down_copy(mo).start()
-
-    forward_copy(mo).start()
+    for h in range(PIECES):
+        @pl.when(has_up)
+        def _():
+            up_copy(mo, h).start()
+
+        @pl.when(has_down)
+        def _():
+            down_copy(mo, h).start()
+
+        forward_copy(mo, h).start()
 
     feat_copy(me).start()
     feat_copy(partner).start()
@@ -192,7 +195,7 @@
     def logits_of(b, first):
         feat_copy(b).wait()
         part = lax.dot_general(
-            coef_all[b], feat[b], (((1,), (1,)), ((), ())), preferred_element_type=F32
+            coef_all[b].reshape(rep, cols), feat[b], (((1,), (1,)), ((), ())), preferred_element_type=F32
         )
         if first:
             acc[...] = part
@@ -202,7 +205,8 @@
     logits_of(me, True)
 
     def arrived(b):
-        coef_wait(b)
+        for h in range(PIECES):
+            coef_wait(b, h)
         logits_of(b, False)
 
     @pl.loop(1, outer)
@@ -210,25 +214,26 @@
         below = mo - i
         above = mo + i
 
-        @pl.when(below >= 0)
-        def _():
-            coef_wait(block(below, mx))
-
-            @pl.when(has_up)
+        for h in range(PIECES):
+            @pl.when(below >= 0)
             def _():
-                up_copy(below).start()
-
-            forward_copy(below).start()
-
-        @pl.when(above < outer)
-        def _():
-            coef_wait(block(above, mx))
-
-            @pl.when(has_down)
+                coef_wait(block(below, mx), h)
+
+                @pl.when(has_up)
+                def _():
+                    up_copy(below, h).start()
+
+                forward_copy(below, h).start()
+
+            @pl.when(above < outer)
             def _():
-                down_copy(above).start()
-
-            forward_copy(above).start()
+                coef_wait(block(above, mx), h)
+
+                @pl.when(has_down)
+                def _():
+                    down_copy(above, h).start()
+
+                forward_copy(above, h).start()
 
         @pl.when(below >= 0)
         def _():
@@ -313,15 +318,19 @@
     def x_copy(o, k):
         return remote(xsend.at[o, k], xrecv.at[o, k], x_send.at[o, k], x_recv.at[o, k], partner)
 
-    def z_up(o, k):
-        return remote(zsend.at[o, k], zrecv.at[o, k], z_send.at[o, k], z_recv.at[o, k], block(mo + 1, mx))
-
-    def z_down(o, k):
+    def z_direct(o):
+        return remote(zsend.at[o, 0], zrecv.at[mo, 0], z_send.at[o, 0], z_recv.at[mo, 0], block(o, mx))
+
+    def z_up(o):
+        return remote(zsend.at[o, 1], zrecv.at[o, 1], z_send.at[o, 1], z_recv.at[o, 1], block(mo + 1, mx))
+
+    def z_down(o):
         slot = jnp.where(o == mo - 1, outer, o)
-        return remote(zsend.at[o, k], zrecv.at[slot, k], z_send.at[o, k], z_recv.at[slot, k], block(mo - 1, mx))
-
-    def z_wait(slot, k):
+        return remote(zsend.at[o, 1], zrecv.at[slot, 1], z_send.at[o, 1], z_recv.at[slot, 1], block(mo - 1, mx))
+
+    def add_in(o, slot, k):
         remote(zsend.at[0, k], zrecv.at[slot, k], z_send.at[0, k], z_recv.at[slot, k], partner).wait_recv()
+        keep[o, k] += zrecv[slot, k].astype(F32)
 
     def products(b, k):
         if k == 0:
@@ -336,28 +345,26 @@
         for k in range(2):
             keep[o, k] = products(block(o, mx), k)
 
-    def add_in(o, slot, k):
-        z_wait(slot, k)
-        keep[o, k] += zrecv[slot, k].astype(F32)
-
     def pass_on(o):
-        for k in range(2):
-            x_copy(o, k).wait_recv()
-            keep[o, k] += xrecv[o, k].astype(F32)
-
-            @pl.when(jnp.logical_or(jnp.logical_and(o > mo, has_down), jnp.logical_and(o < mo, has_up)))
-            def _():
-                add_in(o, o, k)
-
-            zsend[o, k] = keep[o, k].astype(BF16)
-
-            @pl.when(o > mo)
-            def _():
-                z_up(o, k).start()
-
-            @pl.when(o < mo)
-            def _():
-                z_down(o, k).start()
+        x_copy(o, 0).wait_recv()
+        zsend[o, 0] = (keep[o, 0] + xrecv[o, 0].astype(F32)).astype(BF16)
+        z_direct(o).start()
+        x_copy(o, 1).wait_recv()
+        keep[o, 1] += xrecv[o, 1].astype(F32)
+
+        @pl.when(jnp.logical_or(jnp.logical_and(o > mo, has_down), jnp.logical_and(o < mo, has_up)))
+        def _():
+            add_in(o, o, 1)
+
+        zsend[o, 1] = keep[o, 1].astype(BF16)
+
+        @pl.when(o > mo)
+        def _():
+            z_up(o).start()
+
+        @pl.when(o < mo)
+        def _():
+            z_down(o).start()
 
     compute(target_of(0))
     first_sums()
@@ -396,13 +403,17 @@
         x_copy(mo, k).wait_recv()
         keep[mo, k] += xrecv[mo, k].astype(F32)
 
-        @pl.when(has_down)
-        def _():
-            add_in(mo, mo, k)
-
-        @pl.when(has_up)
-        def _():
-            add_in(mo, outer, k)
+    @pl.loop(1, outer)
+    def _(i):
+        add_in(mo, lax.rem(mo + i, outer), 0)
+
+    @pl.when(has_down)
+    def _():
+        add_in(mo, mo, 1)
+
+    @pl.when(has_up)
+    def _():
+        add_in(mo, outer, 1)
 
     grad_ref[...] = keep[mo, 0].T
     hess_ref[...] = keep[mo, 1].T
@@ -413,31 +424,36 @@
 
     @pl.loop(0, outer)
     def _(o):
-        forward_copy(o).wait_send()
+        for h in range(PIECES):
+            forward_copy(o, h).wait_send()
         for k in range(2):
             x_copy(o, k).wait_send()
 
+        @pl.when(o != mo)
+        def _():
+            z_direct(o).wait_send()
+
         @pl.when(has_up)
         def _():
             @pl.when(o <= mo)
             def _():
-                up_copy(o).wait_send()
+                for h in range(PIECES):
+                    up_copy(o, h).wait_send()
 
             @pl.when(o > mo)
             def _():
-                for k in range(2):
-                    z_up(o, k).wait_send()
+                z_up(o).wait_send()
 
         @pl.when(has_down)
         def _():
             @pl.when(o >= mo)
             def _():
-                down_copy(o).wait_send()
+                for h in range(PIECES):
+                    down_copy(o, h).wait_send()
 
             @pl.when(o < mo)
             def _():
-                for k in range(2):
-                    z_down(o, k).wait_send()
+                z_down(o).wait_send()
 
 
 def local(n, features, coefficients, multiplicity, treated, outcome, offset, trim_low, trim_high):
@@ -465,7 +481,7 @@
             pltpu.VMEM((1, rows), F32),
             pltpu.VMEM((1, rep), jnp.int32),
             pltpu.VMEM((1, rep), jnp.int32),
-            pltpu.VMEM((n, rep, cols), BF16),
+            pltpu.VMEM((n, PIECES, rep // PIECES, cols), BF16),
             pltpu.VMEM((rep, rows), F32),
             pltpu.VMEM((rep, rows), F32),
             pltpu.VMEM((rep, rows), F32),
@@ -483,10 +499,10 @@
             dma(()),
             dma(()),
             dma((5,)),
-            dma((outer,)),
-            dma((outer,)),
-            dma((outer,)),
-            dma((n,)),
+            dma((outer, PIECES)),
+            dma((outer, PIECES)),
+            dma((outer, PIECES)),
+            dma((n, PIECES)),
             dma((outer, 2)),
             dma((outer, 2)),
             dma((outer, 2)),

time: 54.9 us -> 53.6 us (0.976)
  Pallas kernels: 50.9 us -> 49.6 us
    pallas_call x1, Pallas kernels: 50.9 us -> 49.6 us  [local(): pl.pallas_call(functools.partial(kernel, n), out_shape=(jax.ShapeDtypeStr...]
where the time goes in v3:
time: 53.6 us; the launch traced here: 53.4 us
  Pallas kernels  49.6 us (93%)
  other arithmetic  1.89 us (4%)
  local copies, waits for them, and re-layouts  1.28 us (2%)
  between operations  0.66 us (1%)
    pallas_call x1, Pallas kernels, local(): pl.pallas_call(functools.partial(kernel, n), out_shape=(jax.ShapeDtypeStr...  49.6 us
    div x1, other arithmetic, local(): score = grad / jnp.sqrt(hess)  1.89 us
    dynamic_slice x1, local copies, waits for them, and re-layouts, local(): lax.dynamic_slice_in_dim(eff, lax.axis_index('row') * owned, owned, axis=1)  1.27 us

profile of v3, /device:TPU:0, one launch (start us, length us, event | category | flops | bytes accessed | tf_op | source)
XLA Modules:
  0.0 53.4 jit_solution(7129535756759101031)
XLA Ops:
  0.6 0.0 copy-start
  0.6 49.6 %propensity.1 = (f32[512,128]{1,0:T(8,128)}, f32[512,128]{1,0:T(8,128)}, f32[2,128]{1,0:T(2,128)}) custom-call(bf16[2048,4096]{1,0:T(8,128)(2,1)} %feat_hbm.1, s32[2048,128]{1,0:T(8,128)} %mult_hbm.1, bf16[512,128]{1,0:T(8,128)(2,1)} %coef_hbm.1, s32[1,2048]{1,0:T(1,128)} %bitcast.8, s32[1,2048]{1,0:T(1,128)} %bitcast.9, f32[1,2048]{1,0:T(1,128)} %bitcast.10, ...), custom_call_target="tpu_custom_call" | custom-call | tf_op jit(solution)/shard_map/propensity/pallas_call | solution.py:466
  50.3 1.3 %constant_dynamic-slice_fusion = f32[2,16]{1,0:T(2,128)} fusion(f32[2,128]{1,0:T(2,128)} %get-tuple-element.8, s32[]{:T(128)S(6)} %select_n.3), kind=kLoop, calls=%fused_computation.2 | loop fusion | bytes 260 | tf_op jit(solution)/shard_map/dynamic_slice | solution.py:531
  51.6 0.0 copy-done
  51.6 1.9 %rsqrt_multiply_fusion = (f32[512,128]{1,0:T(8,128)}, f32[512,128]{1,0:T(8,128)}) fusion(f32[512,128]{1,0:T(8,128)} %get-tuple-element.6, f32[512,128]{1,0:T(8,128)} %get-tuple-element.7, bf16[512,128]{1,0:T(8,128)(2,1)S(1)} %copy-done), kind=kLoop, calls=%fused_computation | loop fusion | flops 327680 | bytes 1179648 | tf_op jit(solution)/shard_map/div | solution.py:529
Async XLA Ops:
  0.6 50.9 %copy-start = (bf16[512,128]{1,0:T(8,128)(2,1)S(1)}, bf16[512,128]{1,0:T(8,128)(2,1)}, u32[]{:S(2)}) copy-start(bf16[512,128]{1,0:T(8,128)(2,1)} %coef_hbm.1) | copy-start | bytes 393220
